TPU v7x, 256 devices: a whole 4x4x8 slice. The times are simulated.
256 devices in a mesh: tile: 32 (over x, z), slide: 8 (over y, core).
Axes of the slice: x: 4, y: 4, z: 8, core: 2. Of those that a mesh axis runs over, the one named last changes fastest.
Arguments:
- tiles: bfloat16 [8, 96, 7, 7, 2048], P('slide', 'tile'), may hold values from -6 to 6
- tile_counts: int32 [8, 32], P('slide', 'tile'), may hold values from 1 to 3, as said below
- tile_weights: float32 [8, 96], P('slide', 'tile'), may hold values from 0.1 to 2
- slide_of: int32 [8, 96, 1], P('slide', 'tile'), may hold values from 0 to 31, as said below
- owner_map: int32 [8, 32], P('slide'), may hold values from 0 to 31, each once within a row
- cotangent: bfloat16 [8, 32, 2048], P('slide', 'tile'), may hold values from -6 to 6
- conv_weight: bfloat16 [9, 64, 2048], replicated, may hold values from -0.25 to 0.25
Outputs:
- pooled: float32 [8, 32, 2048], P('slide', 'tile')
- input_grads: float32 [8, 96, 7, 7, 2048], P('slide', 'tile')
- weight_grads: float32 [9, 64, 2048], P(None, None, 'tile')
Inputs may be any that keep to these rules, and one draw needn't show every extreme that they name: On every device the live tiles are the first tile_counts slots; in each slide group one device has all 3 slots live. `slide_of`: in each slide group, max(1, 8) slides name exactly one slot each, the first slot of some device; the other slots name the remaining slides evenly at random.
All inputs are finite; a program needn't handle non-finite values.
Results may differ from a plain program's by a relative error of at most 0.0065.
Values may be sent and summed in bfloat16 or wider, within the bound.
A program may use at most 128 MiB of HBM per device.

v0:
```python
import jax
import jax.numpy as jnp
from jax import lax
from jax.sharding import PartitionSpec as P

loss_scale = 512.0


def conv_forward(features, weight):
    count_rows, spatial = (features.shape[0], features.shape[1])
    group_width, channels = (weight.shape[1], weight.shape[2])
    groups = channels // group_width
    padded = jnp.pad(features, ((0, 0), (1, 1), (1, 1), (0, 0)))
    summed = jnp.zeros((count_rows, spatial, spatial, groups, group_width), jnp.float32)
    for offset in range(9):
        row_off, col_off = divmod(offset, 3)
        window = padded[:, row_off : row_off + spatial, col_off : col_off + spatial, :].reshape(
            count_rows, spatial, spatial, groups, group_width
        )
        tap = weight[offset].reshape(group_width, groups, group_width)
        summed = summed + jnp.einsum(
            "nhwgi,igo->nhwgo", window, tap, preferred_element_type=jnp.float32
        )
    return summed.reshape(count_rows, spatial, spatial, channels)


def conv_backward(features, weight, pre_grad):
    count_rows, spatial = (features.shape[0], features.shape[1])
    group_width, channels = (weight.shape[1], weight.shape[2])
    groups = channels // group_width
    padded = jnp.pad(features, ((0, 0), (1, 1), (1, 1), (0, 0)))
    grads_split = pre_grad.reshape(count_rows, spatial, spatial, groups, group_width)
    grads_padded = jnp.pad(grads_split, ((0, 0), (1, 1), (1, 1), (0, 0), (0, 0)))
    summed = jnp.zeros((count_rows, spatial, spatial, groups, group_width), jnp.float32)
    pieces = []
    for offset in range(9):
        row_off, col_off = divmod(offset, 3)
        window = padded[:, row_off : row_off + spatial, col_off : col_off + spatial, :].reshape(
            count_rows, spatial, spatial, groups, group_width
        )
        tap = weight[offset].reshape(group_width, groups, group_width)
        pieces.append(
            jnp.einsum(
                "nhwgi,nhwgo->igo", window, grads_split, preferred_element_type=jnp.float32
            ).reshape(group_width, channels)
        )
        shifted = grads_padded[
            :, 2 - row_off : 2 - row_off + spatial, 2 - col_off : 2 - col_off + spatial
        ]
        summed = summed + jnp.einsum(
            "nhwgo,igo->nhwgi", shifted, tap, preferred_element_type=jnp.float32
        )
    input_grads = summed.reshape(count_rows, spatial, spatial, channels)
    return (input_grads, jnp.stack(pieces, axis=0))


def shards(tiles, tile_counts, tile_weights, slide_of, owner_map, cotangent, conv_weight):
    features = tiles[0]
    slots = features.shape[0]
    spatial = features.shape[1]
    tile_total = lax.axis_size("tile")
    my_index = lax.axis_index("tile")
    alive = (jnp.arange(slots, dtype=jnp.int32) < tile_counts[0, 0]).astype(jnp.float32)
    tile_coef = alive * tile_weights[0]
    owner_ids = jnp.arange(tile_total, dtype=jnp.int32)
    slide_hits = slide_of[0, :, 0][:, None] == owner_ids[None, :]
    target = jnp.sum(jnp.where(slide_hits, owner_map[0][None, :], 0), axis=1)
    routing = (target[None, :] == owner_ids[:, None]).astype(jnp.float32) * tile_coef[None, :]
    pre = conv_forward(features, conv_weight)
    embedding = jnp.mean(jax.nn.silu(pre), axis=(1, 2)).astype(jnp.bfloat16)
    shares = lax.all_gather(routing, "tile", axis=1, tiled=True)
    own_row = lax.dynamic_slice_in_dim(shares, my_index, 1, 0)
    numerator = jnp.dot(
        own_row,
        lax.all_gather(embedding, "tile", axis=0, tiled=True).astype(jnp.float32),
        precision=lax.Precision.HIGHEST,
    )
    weight_total = jnp.sum(own_row, axis=1)
    denominator = jnp.maximum(weight_total, 1.0)
    pooled = numerator / denominator[:, None]
    scaled = (loss_scale * cotangent[0].astype(jnp.float32) / denominator[:, None]).astype(
        jnp.bfloat16
    )
    every_scaled = lax.all_gather(scaled, "tile", axis=0, tiled=True)
    tile_grads = jnp.dot(
        routing.T, every_scaled.astype(jnp.float32), precision=lax.Precision.HIGHEST
    )
    sigma = jax.nn.sigmoid(pre)
    slope = sigma * (1.0 + pre * (1.0 - sigma))
    pre_grad = (tile_grads[:, None, None, :] / (spatial * spatial) * slope).astype(jnp.bfloat16)
    input_grads, weight_terms = conv_backward(features, conv_weight, pre_grad)
    shard_sum = lax.psum_scatter(weight_terms, "tile", scatter_dimension=2, tiled=True)
    reduced = lax.psum(shard_sum, "slide")
    return (pooled[None], input_grads[None], reduced / loss_scale)


def solution(mesh):
    return jax.shard_map(
        shards,
        mesh=mesh,
        in_specs=(
            P("slide", "tile", None, None, None),
            P("slide", "tile"),
            P("slide", "tile"),
            P("slide", "tile", None),
            P("slide", None),
            P("slide", "tile", None),
            P(),
        ),
        out_specs=(
            P("slide", "tile", None),
            P("slide", "tile", None, None, None),
            P(None, None, "tile"),
        ),
        check_vma=False,
    )
```

profile of v0, /device:TPU:2, one launch (start us, length us, event | category | flops | bytes accessed | tf_op | source)
XLA Modules:
  0.0 547.1 jit_solution(8483302812085023196)
XLA Ops:
  9.5 51.4 %all-gather.1 = f32[32,3,32]{2,1,0:T(4,128)S(1)} all-gather(f32[1,3,32]{2,1,0:T(4,128)S(1)} %select_bitcast_fusion), channel_id=1, replica_groups=mesh['tile'=32,'slide'=8] {'tile'}, dimensions={0}, use_global_device_ids=true | all-gather | bytes 12672 | tf_op jit(solution)/shard_map/all_gather | solution.py:71
  63.0 47.3 %all-gather = bf16[32,1,2048]{2,1,0:T(2,128)(2,1)S(1)} all-gather(bf16[1,1,2048]{2,1,0:T(2,128)(2,1)S(1)} %divide_convert_fusion), channel_id=2, replica_groups=mesh['tile'=32,'slide'=8] {'tile'}, dimensions={0}, use_global_device_ids=true | all-gather | bytes 135168 | tf_op jit(solution)/shard_map/all_gather | solution.py:84
  125.8 2.5 pad_slice_fusion.12
  128.4 3.0 reshape.109
  139.3 3.3 reshape.113
  142.6 3.0 reshape.114
  145.6 3.2 reshape.106
  148.8 4.0 fusion.33
  161.1 2.9 fusion.38
  164.1 6.7 %multiply_convert_fusion = (bf16[3,7,7,32,64]{4,2,1,0,3:T(8,128)(2,1)S(1)}, f32[3,32,64]{2,0,1:T(4,128)S(1)}) fusion(f32[3,32,64]{2,0,1:T(4,128)S(1)} %copy.348, f32[32,3,7,7,64]{4,3,2,1,0:T(8,128)S(1)} %fusion.25, f32[32,3,7,7,64]{4,3,2,1,0:T(8,128)S(1)} %fusion.27, f32[32,3,7,7,64]{4,3,2,1,0:T(8,128)S(1)} %fusion.29, ...), kind=kOutput, calls=%fused_computation.22 | convolution fusion | flops 44249088 | bytes 11149312 | tf_op jit(solution)/shard_map/nhwgi,igo->nhwgo/dot_general | solution.py:21
  170.8 4.2 fusion.21
  175.0 2.4 fusion.19
  179.9 2.4 fusion.15
  182.3 2.4 fusion.13
  184.8 2.4 fusion.11
  187.2 2.6 fusion.9
  189.8 2.5 fusion.7
  221.8 12.9 %copy.450 = f32[9,64,2048]{1,0,2:T(8,128)} copy(f32[9,64,2048]{2,1,0:T(8,128)} %constant_dynamic-update-slice_fusion) | data formatting | bytes 9437184
  234.7 12.6 %reshape.153 = f32[2048,576]{1,0:T(8,128)} reshape(f32[2048,9,64]{2,1,0:T(8,128)} %bitcast.128) | data formatting | bytes 9437184
  247.5 48.3 %all-gather.2 = bf16[32,3,2048]{2,1,0:T(4,128)(2,1)S(1)} all-gather(bf16[1,3,2048]{2,1,0:T(4,128)(2,1)S(1)} %reshape.118), channel_id=1, replica_groups=mesh['tile'=32,'slide'=8] {'tile'}, dimensions={0}, use_global_device_ids=true | all-gather | bytes 405504 | tf_op jit(solution)/shard_map/all_gather | solution.py:75
  307.2 5.6 %add_bitcast_fusion = f32[3,7,7,32,64]{4,2,1,0,3:T(8,128)} fusion(f32[32,3,7,7,64]{4,3,2,1,0:T(8,128)S(1)} %fusion.6, f32[32,3,7,7,64]{4,3,2,1,0:T(8,128)S(1)} %fusion.5, f32[32,3,7,7,64]{4,3,2,1,0:T(8,128)S(1)} %fusion.4, f32[32,3,7,7,64]{4,3,2,1,0:T(8,128)} %fusion.50, f32[32,3,7,7,64]{4,3,2,1,0:T(8,128)S(1)} %fusion.3, ...), kind=kOutput, calls=%fused_computation.21 | convolution fusion | flops 40943616 | bytes 11702272 | tf_op jit(solution)/shard_map/nhwgo,igo->nhwgi/dot_general | solution.py:50
  312.8 158.3 %reduce-scatter.4.cloned.1.call-done = f32[64,576]{1,0:T(8,128)} async-done(((f32[2048,576]{1,0:T(8,128)}), f32[64,576]{1,0:T(8,128)}) %reduce-scatter.4.cloned.1.call-update) | async-done | bytes 147472
  475.8 2.5 broadcast_in_dim_reshape.4
  478.3 60.0 %all-reduce.4.cloned.1.call-done = f32[9,64,64]{2,1,0:T(8,128)} async-done(((f32[9,64,64]{2,1,0:T(8,128)}), f32[9,64,64]{2,1,0:T(8,128)}) %all-reduce.4.cloned.1.call-update) | async-done | bytes 147472 | tf_op jit(solution)/shard_map/psum | solution.py:93
  (135 shorter events, 84.4 us)
Async XLA Ops:
  7.2 103.5 %copy-start.23 = (bf16[1,3,7,7,2048]{4,3,2,1,0:T(8,128)(2,1)S(1)}, bf16[1,3,7,7,2048]{4,3,2,1,0:T(8,128)(2,1)}, u32[]{:S(2)}) copy-start(bf16[1,3,7,7,2048]{4,3,2,1,0:T(8,128)(2,1)} %param.7) | copy-start | bytes 1806340
  7.2 463.9 %reduce-scatter.4.cloned.1.call-start = ((), (), s32[]{:S(2)}) async-start(), calls=%async_computation.2 | async-start | bytes 5406720
  128.4 3.1 copy-start.24
  139.3 17.7 %copy-start = (bf16[3,7,7,32,64]{4,3,2,1,0:T(8,128)(2,1)}, bf16[3,7,7,32,64]{4,3,2,1,0:T(8,128)(2,1)S(1)}, u32[]{:S(2)}) copy-start(bf16[3,7,7,32,64]{4,3,2,1,0:T(8,128)(2,1)S(1)} %reshape.112) | copy-start | bytes 1806340
  148.8 4.0 copy-start.4
  148.8 4.0 copy-start.15
  152.8 1.4 copy-start.3
  152.8 1.4 copy-start.13
  154.2 1.4 copy-start.2
  154.2 1.4 copy-start.19
  159.7 1.4 copy-start.21
  170.8 4.3 copy-start.8
  175.0 2.5 copy-start.9
  177.5 2.4 copy-start.31
  182.3 2.4 copy-start.1
  189.8 2.5 copy-start.5
  212.1 3.9 copy-start.30
  212.1 4.8 copy-start.29
  214.1 3.6 copy-start.28
  216.0 2.5 copy-start.27
  216.8 2.5 copy-start.26
  247.4 49.1 %copy-start.22 = (bf16[64,32,64]{2,1,0:T(8,128)(2,1)S(1)}, bf16[64,32,64]{2,1,0:T(8,128)(2,1)}, u32[]{:S(2)}) copy-start(bf16[64,32,64]{2,1,0:T(8,128)(2,1)} %reshape_squeeze.37) | copy-start | bytes 786436
  247.4 291.0 %all-reduce.4.cloned.1.call-start = ((), (), s32[]{:S(2)}) async-start(), calls=%async_computation.1 | async-start | bytes 589824 | tf_op jit(solution)/shard_map/psum | solution.py:93
  304.7 2.4 copy-start.14
  (10 other events, 12.4 us)
Sparse Core Ops, SparseCore 0:
  247.5 223.5 reduce-scatter.3
  474.0 64.3 all-reduce.3
where the time goes:
time: 554 us; the launch traced here: 547 us
  waiting for transfers between devices  218 us (39%)
  blocking collectives  147 us (27%)
  local copies, waits for them, and re-layouts  99.3 us (18%)
  matrix products  61.1 us (11%)
  between operations  16 us (3%)
    unnamed x3, waiting for transfers between devices  158 us
    psum x1, waiting for transfers between devices, shards(): reduced = lax.psum(shard_sum, 'slide')  60 us
    all_gather x1, blocking collectives, shards(): shares = lax.all_gather(routing, 'tile', axis=1, tiled=True)  51.4 us
    all_gather x1, blocking collectives, shards(): lax.all_gather(embedding, 'tile', axis=0, tiled=True).astype(jnp.float32)  48.3 us
    all_gather x1, blocking collectives, shards(): every_scaled = lax.all_gather(scaled, 'tile', axis=0, tiled=True)  47.3 us
    unnamed x79, local copies, waits for them, and re-layouts  37.3 us
    dot_general x9, matrix products, conv_backward(): jnp.einsum('nhwgi,nhwgo->igo', window, grads_split, preferred_element_typ...  22.9 us
    reshape x9, local copies, waits for them, and re-layouts, conv_forward(): padded[:, row_off:row_off + spatial, col_off:col_off + spatial, :]  22.6 us
  transfers between devices with their start and end apart: 2, of which 2 were waited for; matrix products, arithmetic and copies ran while one was open for 4% of the time, Pallas kernels for 0%

commit v1 on v0

--- a/solution.py
+++ b/solution.py
@@ -90,7 +90,7 @@
     pre_grad = (tile_grads[:, None, None, :] / (spatial * spatial) * slope).astype(jnp.bfloat16)
     input_grads, weight_terms = conv_backward(features, conv_weight, pre_grad)
     shard_sum = lax.psum_scatter(weight_terms, "tile", scatter_dimension=2, tiled=True)
-    reduced = lax.psum(shard_sum, "slide")
+    reduced = jnp.sum(lax.all_gather(shard_sum, "slide"), axis=0)
     return (pooled[None], input_grads[None], reduced / loss_scale)
 
 

time: 554 us -> 518 us (0.935)
  waiting for transfers between devices: 218 us -> 170 us
  local copies, waits for them, and re-layouts: 99.3 us -> 105 us
  matrix products: 61.1 us -> 66.7 us
    psum x1 -> x0, waiting for transfers between devices: 60 us -> none  [shards(): reduced = lax.psum(shard_sum, 'slide')]
    all_gather x0 -> x1, waiting for transfers between devices: none -> 11.1 us  [shards(): reduced = jnp.sum(lax.all_gather(shard_sum, 'slide'), axis=0)]
    dot_general x9, matrix products: 15.9 us -> 24.2 us  [conv_backward(): jnp.einsum('nhwgo,igo->nhwgi', shifted, tap, preferred_element_type=jnp.f...]
    unnamed x79 -> x91, local copies, waits for them, and re-layouts: 37.3 us -> 42.2 us
  transfers between devices with their start and end apart: 2 -> 2, of which waited for: 2 -> 2; matrix products, arithmetic and copies ran while one was open for 4% -> 6% of each run, Pallas kernels for 0% -> 0%
where the time goes in v1:
time: 518 us; the launch traced here: 510 us
  waiting for transfers between devices  170 us (33%)
  blocking collectives  147 us (28%)
  local copies, waits for them, and re-layouts  105 us (20%)
  matrix products  66.7 us (13%)
  between operations  16 us (3%)
  other arithmetic  5.58 us (1%)
    unnamed x3, waiting for transfers between devices  159 us
    all_gather x1, blocking collectives, shards(): shares = lax.all_gather(routing, 'tile', axis=1, tiled=True)  51.4 us
    all_gather x1, blocking collectives, shards(): lax.all_gather(embedding, 'tile', axis=0, tiled=True).astype(jnp.float32)  48.1 us
    all_gather x1, blocking collectives, shards(): every_scaled = lax.all_gather(scaled, 'tile', axis=0, tiled=True)  47.3 us
    unnamed x91, local copies, waits for them, and re-layouts  42.2 us
    dot_general x9, matrix products, conv_backward(): jnp.einsum('nhwgo,igo->nhwgi', shifted, tap, preferred_element_type=jnp.f...  24.2 us
    dot_general x9, matrix products, conv_backward(): jnp.einsum('nhwgi,nhwgo->igo', window, grads_split, preferred_element_typ...  22.7 us
    reshape x9, local copies, waits for them, and re-layouts, conv_forward(): padded[:, row_off:row_off + spatial, col_off:col_off + spatial, :]  22.5 us
  transfers between devices with their start and end apart: 2, of which 2 were waited for; matrix products, arithmetic and copies ran while one was open for 6% of the time, Pallas kernels for 0%

profile of v1, /device:TPU:2, one launch (start us, length us, event | category | flops | bytes accessed | tf_op | source)
XLA Modules:
  0.0 509.7 jit_solution(6165199759344250239)
XLA Ops:
  9.5 51.4 %all-gather.2 = f32[32,3,32]{2,1,0:T(4,128)S(1)} all-gather(f32[1,3,32]{2,1,0:T(4,128)S(1)} %select_bitcast_fusion), channel_id=1, replica_groups=mesh['tile'=32,'slide'=8] {'tile'}, dimensions={0}, use_global_device_ids=true | all-gather | bytes 12672 | tf_op jit(solution)/shard_map/all_gather | solution.py:71
  63.0 47.3 %all-gather = bf16[32,1,2048]{2,1,0:T(2,128)(2,1)S(1)} all-gather(bf16[1,1,2048]{2,1,0:T(2,128)(2,1)S(1)} %divide_convert_fusion), channel_id=2, replica_groups=mesh['tile'=32,'slide'=8] {'tile'}, dimensions={0}, use_global_device_ids=true | all-gather | bytes 135168 | tf_op jit(solution)/shard_map/all_gather | solution.py:84
  128.2 3.0 reshape.109
  139.1 3.3 reshape.113
  142.4 3.0 reshape.114
  145.3 3.2 reshape.106
  148.5 4.0 fusion.33
  162.2 5.8 %multiply_convert_fusion = (bf16[3,7,7,32,64]{4,2,1,0,3:T(8,128)(2,1)S(1)}, f32[3,32,64]{2,0,1:T(4,128)S(1)}) fusion(f32[3,32,64]{2,0,1:T(4,128)S(1)} %copy.387, f32[32,3,7,7,64]{4,3,2,1,0:T(8,128)S(1)} %fusion.25, f32[32,3,7,7,64]{4,3,2,1,0:T(8,128)S(1)} %fusion.27, f32[32,3,7,7,64]{4,3,2,1,0:T(8,128)S(1)} %fusion.29, ...), kind=kOutput, calls=%fused_computation.22 | convolution fusion | flops 44249088 | bytes 11149312 | tf_op jit(solution)/shard_map/nhwgi,igo->nhwgo/dot_general | solution.py:21
  168.1 4.3 fusion.21
  174.7 2.5 fusion.17
  177.2 2.4 fusion.15
  179.7 2.5 fusion.13
  187.0 2.4 fusion.7
  218.9 13.0 %copy.491 = f32[9,64,2048]{1,0,2:T(8,128)} copy(f32[9,64,2048]{2,1,0:T(8,128)} %constant_dynamic-update-slice_fusion) | data formatting | bytes 9437184
  232.0 12.6 %reshape.154 = f32[2048,576]{1,0:T(8,128)} reshape(f32[2048,9,64]{2,1,0:T(8,128)} %bitcast.129) | data formatting | bytes 9437184
  244.7 48.1 %all-gather.3 = bf16[32,3,2048]{2,1,0:T(4,128)(2,1)S(1)} all-gather(bf16[1,3,2048]{2,1,0:T(4,128)(2,1)S(1)} %reshape.119), channel_id=1, replica_groups=mesh['tile'=32,'slide'=8] {'tile'}, dimensions={0}, use_global_device_ids=true | all-gather | bytes 405504 | tf_op jit(solution)/shard_map/all_gather | solution.py:75
  296.3 2.8 fusion.2
  299.1 2.9 fusion.3
  301.9 2.8 fusion.4
  304.8 2.8 fusion.5
  310.0 158.5 %reduce-scatter.4.cloned.1.call-done = f32[64,576]{1,0:T(8,128)} async-done(((f32[2048,576]{1,0:T(8,128)}), f32[64,576]{1,0:T(8,128)}) %reduce-scatter.4.cloned.1.call-update) | async-done | bytes 147472
  475.9 6.1 %add_bitcast_fusion = f32[3,7,7,32,64]{4,2,1,0,3:T(8,128)S(1)} fusion(f32[32,3,7,7,64]{4,3,2,1,0:T(8,128)} %fusion.6, f32[32,3,7,7,64]{4,3,2,1,0:T(8,128)} %fusion.5, f32[32,3,7,7,64]{4,3,2,1,0:T(8,128)} %fusion.4, f32[32,3,7,7,64]{4,3,2,1,0:T(8,128)S(1)} %fusion.50, f32[32,3,7,7,64]{4,3,2,1,0:T(8,128)S(1)} %copy-done.2, ...), kind=kOutput, calls=%fused_computation.21 | convolution fusion | flops 40943616 | bytes 11702272 | tf_op jit(solution)/shard_map/nhwgo,igo->nhwgi/dot_general | solution.py:50
  483.8 3.9 broadcast_in_dim_reshape.4
  488.6 11.1 %all-gather.6.cloned.1.call-done = f32[72,64,64]{2,1,0:T(8,128)} async-done(((f32[9,64,64]{2,1,0:T(8,128)}), f32[72,64,64]{2,1,0:T(8,128)}) %all-gather.6.cloned.1.call-update) | async-done | bytes 1179664 | tf_op jit(solution)/shard_map/all_gather | solution.py:93
  (148 shorter events, 94.2 us)
Async XLA Ops:
  7.2 103.5 %copy-start.28 = (bf16[1,3,7,7,2048]{4,3,2,1,0:T(8,128)(2,1)S(1)}, bf16[1,3,7,7,2048]{4,3,2,1,0:T(8,128)(2,1)}, u32[]{:S(2)}) copy-start(bf16[1,3,7,7,2048]{4,3,2,1,0:T(8,128)(2,1)} %param.7) | copy-start | bytes 1806340
  7.2 461.3 %reduce-scatter.4.cloned.1.call-start = ((), (), s32[]{:S(2)}) async-start(), calls=%async_computation.2 | async-start | bytes 5406720
  139.1 17.7 %copy-start.3 = (bf16[3,7,7,32,64]{4,3,2,1,0:T(8,128)(2,1)}, bf16[3,7,7,32,64]{4,3,2,1,0:T(8,128)(2,1)S(1)}, u32[]{:S(2)}) copy-start(bf16[3,7,7,32,64]{4,3,2,1,0:T(8,128)(2,1)S(1)} %reshape.112) | copy-start | bytes 1806340
  148.5 4.0 copy-start.9
  148.5 4.0 copy-start.15
  168.0 4.3 copy-start.13
  174.7 2.5 copy-start.36
  179.7 2.5 copy-start.4
  209.1 3.9 copy-start.34
  209.1 4.8 copy-start.33
  211.1 3.6 copy-start.32
  213.1 2.5 copy-start.31
  213.9 2.5 copy-start.30
  244.6 49.3 %copy-start.27 = (bf16[64,32,64]{2,1,0:T(8,128)(2,1)S(1)}, bf16[64,32,64]{2,1,0:T(8,128)(2,1)}, u32[]{:S(2)}) copy-start(bf16[64,32,64]{2,1,0:T(8,128)(2,1)} %reshape_squeeze.37) | copy-start | bytes 786436
  244.6 255.1 %all-gather.6.cloned.1.call-start = ((), (), s32[]{:S(2)}) async-start(), calls=%async_computation.1 | async-start | bytes 2654208 | tf_op jit(solution)/shard_map/all_gather | solution.py:93
  296.3 2.8 copy-start.19
  299.1 2.9 copy-start.21
  301.9 2.8 copy-start.18
  304.8 2.8 copy-start.25
  307.6 165.8 %copy-start.29 = (bf16[64,32,64]{2,1,0:T(8,128)(2,1)S(1)}, bf16[64,32,64]{2,1,0:T(8,128)(2,1)}, u32[]{:S(2)}) copy-start(bf16[64,32,64]{2,1,0:T(8,128)(2,1)} %reshape_squeeze.40) | copy-start | bytes 786436
  310.0 162.2 %copy-start.16 = (bf16[64,32,64]{2,1,0:T(8,128)(2,1)S(1)}, bf16[64,32,64]{2,1,0:T(8,128)(2,1)}, u32[]{:S(2)}) copy-start(bf16[64,32,64]{2,1,0:T(8,128)(2,1)} %reshape_squeeze.36) | copy-start | bytes 786436
  472.2 2.6 copy-start.2
  473.4 2.4 copy-start
  483.8 3.9 copy-start.35
  (15 other events, 26.6 us)
Sparse Core Ops, SparseCore 0:
  244.7 223.7 reduce-scatter.3
  472.3 27.3 all-gather.5
